TPU v7x, 512 devices: a whole 4x8x8 slice. The times are simulated.
512 devices in a mesh: samp: 32 (over x_hi, y, core), feat: 16 (over x_lo, z).
Axes of the slice: x: 4 (x_hi: 2, x_lo: 2; x = x_hi * 2 + x_lo), y: 8, z: 8, core: 2. Of those that a mesh axis runs over, the one named last changes fastest.
Arguments:
- labels: int32 [2097152], P('samp'), may hold values 0 or 1
- beta: float32 [1048576], P('feat'), may hold values from -1.2 to 1.2
- tile_rows: int32 [32, 16, 64], P('samp', 'feat'), may hold values from 0 to 511, as said below
- tile_cols: int32 [32, 16, 64], P('samp', 'feat'), may hold values from 0 to 511, as said below
- tile_values: bfloat16 [32, 16, 64, 128, 128], P('samp', 'feat'), may hold values from -0.5 to 0.5
- block_order: int32 [16, 16], P('feat'), may hold values from 0 to 511, as said below
- hess_inv: float32 [16, 16, 128, 128], P('feat')
Outputs:
- beta_new: float32 [1048576], P('feat')
- residual: float32 [2097152], P(('samp', 'feat'))
Inputs may be any that keep to these rules, and one draw needn't show every extreme that they name: `tile_rows`: row block numbers within a samp index. `tile_cols`: feature block numbers within a feat index. Each row of block_order holds 16 distinct block numbers.
All inputs are finite; a program needn't handle non-finite values. No bound on the sum of `labels` on one device may be relied on, other than what follows from the above.
Results may differ from a plain program's by a relative error of at most 0.0025.
Values sent between devices are 32-bit elements; how exact they have to be, the bound alone decides.
A program may use at most 64 MiB of HBM per device.

v0:
```python
import jax
import jax.numpy as jnp
from jax import lax
from jax.sharding import PartitionSpec as P

exact_prec = lax.Precision.HIGHEST
l1_penalty = 0.25


def from_behind(value, axis, steps):
    count = lax.axis_size(axis)
    pairs = [(source, (source + steps) % count) for source in range(count)]
    return lax.ppermute(value, axis, pairs)


def per_device(labels, beta, tile_rows, tile_cols, tile_values, block_order, hess_inv):
    cycle_size = lax.axis_size("feat")
    my_index = lax.axis_index("feat")
    row_ids = tile_rows[0, 0]
    col_ids = tile_cols[0, 0]
    values = tile_values[0, 0]
    tile_edge = values.shape[-1]
    row_blocks = labels.shape[0] // tile_edge
    group_blocks = row_blocks // cycle_size
    blocks = beta.reshape(-1, tile_edge)
    picked = jnp.take(blocks.astype(jnp.bfloat16), col_ids, axis=0)
    products = jnp.einsum("krc,kc->kr", values, picked, preferred_element_type=jnp.float32)
    placing = (row_ids[:, None] == jnp.arange(row_blocks, dtype=jnp.int32)[None, :]).astype(
        jnp.float32
    )
    partial_sum = jnp.dot(placing.T, products, precision=exact_prec)
    margins = lax.psum_scatter(partial_sum, "feat", scatter_dimension=0, tiled=True)
    probability = jax.nn.sigmoid(margins)
    weight = probability * (1.0 - probability)
    own_labels = lax.dynamic_slice_in_dim(
        labels.reshape(row_blocks, tile_edge), my_index * group_blocks, group_blocks, 0
    )
    residual = own_labels.astype(jnp.float32) - probability
    sub_ids = jnp.arange(group_blocks, dtype=jnp.int32)
    inverses = hess_inv[0]
    targets = block_order[0]

    def run_section(section_index, carry):
        blocks, residual, weight = carry
        group_index = (my_index - section_index) % cycle_size
        target = lax.dynamic_index_in_dim(targets, section_index, 0, keepdims=False)
        inverse = lax.dynamic_index_in_dim(inverses, section_index, 0, keepdims=False)
        offsets = row_ids - group_index * group_blocks
        matches = (col_ids == target) & (offsets >= 0) & (offsets < group_blocks)
        chosen = (offsets[:, None] == sub_ids[None, :]) & matches[:, None]
        rounded = residual.astype(jnp.bfloat16)
        resid_tiles = jnp.dot(
            chosen.astype(jnp.bfloat16), rounded, preferred_element_type=jnp.float32
        ).astype(jnp.bfloat16)
        local_grad = jnp.einsum(
            "krc,kr->c", values, resid_tiles, preferred_element_type=jnp.float32
        )
        gradient = lax.psum(local_grad, "samp")
        current = lax.dynamic_index_in_dim(blocks, target, 0, keepdims=False)
        moved_block = current + jnp.dot(inverse, gradient, precision=exact_prec)
        shrunk = jnp.sign(moved_block) * jnp.maximum(jnp.abs(moved_block) - l1_penalty, 0.0)
        change = (shrunk - current).astype(jnp.bfloat16)
        image_rows = jnp.einsum("krc,c->kr", values, change, preferred_element_type=jnp.float32)
        landed = jnp.dot(chosen.astype(jnp.float32).T, image_rows, precision=exact_prec)
        residual = residual - weight * landed
        blocks = lax.dynamic_update_index_in_dim(blocks, shrunk, target, 0)
        residual, weight = from_behind((residual, weight), "feat", 1)
        return (blocks, residual, weight)

    blocks, residual, weight = lax.fori_loop(0, cycle_size, run_section, (blocks, residual, weight))
    return (blocks.reshape(-1), residual.reshape(-1))


def solution(mesh):
    placed = (
        P("samp"),
        P("feat"),
        P("samp", "feat", None),
        P("samp", "feat", None),
        P("samp", "feat", None, None, None),
        P("feat", None),
        P("feat", None, None, None),
    )
    return jax.shard_map(
        per_device,
        mesh=mesh,
        in_specs=placed,
        out_specs=(P("feat"), P(("samp", "feat"))),
        check_vma=False,
    )
```

profile of v0, /device:TPU:1, one launch (start us, length us, event | category | flops | bytes accessed | tf_op | source)
XLA Modules:
  0.0 1390.1 jit_solution(13827757922583052736)
XLA Ops:
  14.4 68.1 %reduce-scatter.2.cloned.1.call-done = f32[32,128]{1,0:T(8,128)} async-done(((f32[512,128]{1,0:T(8,128)}), f32[32,128]{1,0:T(8,128)}) %reduce-scatter.2.cloned.1.call-update) | async-done | bytes 16400 | tf_op jit(solution)/shard_map/reduce_scatter | solution.py:32
  83.2 1299.3 %while.20 = (s32[]{:T(128)}, f32[512,128]{1,0:T(8,128)S(1)}, f32[32,128]{1,0:T(8,128)S(1)}, f32[32,128]{1,0:T(8,128)S(1)}, s32[16]{0:T(128)S(1)}, /*index=5*/f32...) while((s32[]{:T(128)}, f32[512,128]{1,0:T(8,128)S(1)}, ...), condition=%wide.region_3.4_spmd.clone, body=%wide.region_1.3_spmd.clone.sunk | while | flops 8091154 | bytes 4595052 | solution.py:70
  88.4 76.9 %psum.16 = f32[128]{0:T(128)S(1)} all-reduce(f32[128]{0:T(128)S(1)} %convolution_bitcast_fusion.3), channel_id=1, replica_groups=mesh['samp'=32,'feat'=16] {'samp'}, use_global_device_ids=true, to_apply=%region_2.2 | all-reduce | flops 128 | bytes 1024 | tf_op jit(solution)/shard_map/while/body/eval_jaxpr/psum | solution.py:58
  169.9 4.9 collective-permute-done
  179.9 65.9 %psum.16 = f32[128]{0:T(128)S(1)} all-reduce(f32[128]{0:T(128)S(1)} %convolution_bitcast_fusion.3), channel_id=1, replica_groups=mesh['samp'=32,'feat'=16] {'samp'}, use_global_device_ids=true, to_apply=%region_2.2 | all-reduce | flops 128 | bytes 1024 | tf_op jit(solution)/shard_map/while/body/eval_jaxpr/psum | solution.py:58
  250.4 4.9 collective-permute-done
  260.4 65.9 %psum.16 = f32[128]{0:T(128)S(1)} all-reduce(f32[128]{0:T(128)S(1)} %convolution_bitcast_fusion.3), channel_id=1, replica_groups=mesh['samp'=32,'feat'=16] {'samp'}, use_global_device_ids=true, to_apply=%region_2.2 | all-reduce | flops 128 | bytes 1024 | tf_op jit(solution)/shard_map/while/body/eval_jaxpr/psum | solution.py:58
  340.9 65.9 %psum.16 = f32[128]{0:T(128)S(1)} all-reduce(f32[128]{0:T(128)S(1)} %convolution_bitcast_fusion.3), channel_id=1, replica_groups=mesh['samp'=32,'feat'=16] {'samp'}, use_global_device_ids=true, to_apply=%region_2.2 | all-reduce | flops 128 | bytes 1024 | tf_op jit(solution)/shard_map/while/body/eval_jaxpr/psum | solution.py:58
  421.4 65.9 %psum.16 = f32[128]{0:T(128)S(1)} all-reduce(f32[128]{0:T(128)S(1)} %convolution_bitcast_fusion.3), channel_id=1, replica_groups=mesh['samp'=32,'feat'=16] {'samp'}, use_global_device_ids=true, to_apply=%region_2.2 | all-reduce | flops 128 | bytes 1024 | tf_op jit(solution)/shard_map/while/body/eval_jaxpr/psum | solution.py:58
  492.0 4.9 collective-permute-done
  501.9 65.9 %psum.16 = f32[128]{0:T(128)S(1)} all-reduce(f32[128]{0:T(128)S(1)} %convolution_bitcast_fusion.3), channel_id=1, replica_groups=mesh['samp'=32,'feat'=16] {'samp'}, use_global_device_ids=true, to_apply=%region_2.2 | all-reduce | flops 128 | bytes 1024 | tf_op jit(solution)/shard_map/while/body/eval_jaxpr/psum | solution.py:58
  572.5 4.9 collective-permute-done
  582.5 65.9 %psum.16 = f32[128]{0:T(128)S(1)} all-reduce(f32[128]{0:T(128)S(1)} %convolution_bitcast_fusion.3), channel_id=1, replica_groups=mesh['samp'=32,'feat'=16] {'samp'}, use_global_device_ids=true, to_apply=%region_2.2 | all-reduce | flops 128 | bytes 1024 | tf_op jit(solution)/shard_map/while/body/eval_jaxpr/psum | solution.py:58
  663.0 65.9 %psum.16 = f32[128]{0:T(128)S(1)} all-reduce(f32[128]{0:T(128)S(1)} %convolution_bitcast_fusion.3), channel_id=1, replica_groups=mesh['samp'=32,'feat'=16] {'samp'}, use_global_device_ids=true, to_apply=%region_2.2 | all-reduce | flops 128 | bytes 1024 | tf_op jit(solution)/shard_map/while/body/eval_jaxpr/psum | solution.py:58
  743.5 65.9 %psum.16 = f32[128]{0:T(128)S(1)} all-reduce(f32[128]{0:T(128)S(1)} %convolution_bitcast_fusion.3), channel_id=1, replica_groups=mesh['samp'=32,'feat'=16] {'samp'}, use_global_device_ids=true, to_apply=%region_2.2 | all-reduce | flops 128 | bytes 1024 | tf_op jit(solution)/shard_map/while/body/eval_jaxpr/psum | solution.py:58
  824.0 65.9 %psum.16 = f32[128]{0:T(128)S(1)} all-reduce(f32[128]{0:T(128)S(1)} %convolution_bitcast_fusion.3), channel_id=1, replica_groups=mesh['samp'=32,'feat'=16] {'samp'}, use_global_device_ids=true, to_apply=%region_2.2 | all-reduce | flops 128 | bytes 1024 | tf_op jit(solution)/shard_map/while/body/eval_jaxpr/psum | solution.py:58
  904.5 65.9 %psum.16 = f32[128]{0:T(128)S(1)} all-reduce(f32[128]{0:T(128)S(1)} %convolution_bitcast_fusion.3), channel_id=1, replica_groups=mesh['samp'=32,'feat'=16] {'samp'}, use_global_device_ids=true, to_apply=%region_2.2 | all-reduce | flops 128 | bytes 1024 | tf_op jit(solution)/shard_map/while/body/eval_jaxpr/psum | solution.py:58
  985.1 65.9 %psum.16 = f32[128]{0:T(128)S(1)} all-reduce(f32[128]{0:T(128)S(1)} %convolution_bitcast_fusion.3), channel_id=1, replica_groups=mesh['samp'=32,'feat'=16] {'samp'}, use_global_device_ids=true, to_apply=%region_2.2 | all-reduce | flops 128 | bytes 1024 | tf_op jit(solution)/shard_map/while/body/eval_jaxpr/psum | solution.py:58
  1055.6 4.9 collective-permute-done
  1065.6 65.9 %psum.16 = f32[128]{0:T(128)S(1)} all-reduce(f32[128]{0:T(128)S(1)} %convolution_bitcast_fusion.3), channel_id=1, replica_groups=mesh['samp'=32,'feat'=16] {'samp'}, use_global_device_ids=true, to_apply=%region_2.2 | all-reduce | flops 128 | bytes 1024 | tf_op jit(solution)/shard_map/while/body/eval_jaxpr/psum | solution.py:58
  1146.1 65.9 %psum.16 = f32[128]{0:T(128)S(1)} all-reduce(f32[128]{0:T(128)S(1)} %convolution_bitcast_fusion.3), channel_id=1, replica_groups=mesh['samp'=32,'feat'=16] {'samp'}, use_global_device_ids=true, to_apply=%region_2.2 | all-reduce | flops 128 | bytes 1024 | tf_op jit(solution)/shard_map/while/body/eval_jaxpr/psum | solution.py:58
  1226.6 65.9 %psum.16 = f32[128]{0:T(128)S(1)} all-reduce(f32[128]{0:T(128)S(1)} %convolution_bitcast_fusion.3), channel_id=1, replica_groups=mesh['samp'=32,'feat'=16] {'samp'}, use_global_device_ids=true, to_apply=%region_2.2 | all-reduce | flops 128 | bytes 1024 | tf_op jit(solution)/shard_map/while/body/eval_jaxpr/psum | solution.py:58
  1307.1 65.9 %psum.16 = f32[128]{0:T(128)S(1)} all-reduce(f32[128]{0:T(128)S(1)} %convolution_bitcast_fusion.3), channel_id=1, replica_groups=mesh['samp'=32,'feat'=16] {'samp'}, use_global_device_ids=true, to_apply=%region_2.2 | all-reduce | flops 128 | bytes 1024 | tf_op jit(solution)/shard_map/while/body/eval_jaxpr/psum | solution.py:58
  1377.7 4.9 collective-permute-done
  (225 shorter events, 181.0 us)
Async XLA Ops:
  7.2 75.3 %reduce-scatter.2.cloned.1.call-start = ((), (), s32[]{:S(2)}) async-start(), calls=%async_computation.1 | async-start | bytes 278528 | tf_op jit(solution)/shard_map/reduce_scatter | solution.py:32
  83.3 86.6 %collective-permute-start.1 = (f32[32,128]{1,0:T(8,128)S(1)}, f32[32,128]{1,0:T(8,128)S(1)}, u32[]{:S(2)}, u32[]{:S(2)}) collective-permute-start(f32[32,128]{1,0:T(8,128)S(1)} %copy.27), channel_id=1, source_target_pairs={{0,1},{1,2},{2,3},{3,4},{4,5},{5,6},{6,7},{7,8},{8,9},{9,10},{10,1... | collective-permute-start | bytes 49160 | tf_op jit(solution)/shard_map/while/body/eval_jaxpr/ppermute | solution.py:13
  167.9 6.9 collective-permute-start
  174.8 75.6 %collective-permute-start.1 = (f32[32,128]{1,0:T(8,128)S(1)}, f32[32,128]{1,0:T(8,128)S(1)}, u32[]{:S(2)}, u32[]{:S(2)}) collective-permute-start(f32[32,128]{1,0:T(8,128)S(1)} %copy.27), channel_id=1, source_target_pairs={{0,1},{1,2},{2,3},{3,4},{4,5},{5,6},{6,7},{7,8},{8,9},{9,10},{10,1... | collective-permute-start | bytes 49160 | tf_op jit(solution)/shard_map/while/body/eval_jaxpr/ppermute | solution.py:13
  255.3 75.6 %collective-permute-start.1 = (f32[32,128]{1,0:T(8,128)S(1)}, f32[32,128]{1,0:T(8,128)S(1)}, u32[]{:S(2)}, u32[]{:S(2)}) collective-permute-start(f32[32,128]{1,0:T(8,128)S(1)} %copy.27), channel_id=1, source_target_pairs={{0,1},{1,2},{2,3},{3,4},{4,5},{5,6},{6,7},{7,8},{8,9},{9,10},{10,1... | collective-permute-start | bytes 49160 | tf_op jit(solution)/shard_map/while/body/eval_jaxpr/ppermute | solution.py:13
  335.8 75.6 %collective-permute-start.1 = (f32[32,128]{1,0:T(8,128)S(1)}, f32[32,128]{1,0:T(8,128)S(1)}, u32[]{:S(2)}, u32[]{:S(2)}) collective-permute-start(f32[32,128]{1,0:T(8,128)S(1)} %copy.27), channel_id=1, source_target_pairs={{0,1},{1,2},{2,3},{3,4},{4,5},{5,6},{6,7},{7,8},{8,9},{9,10},{10,1... | collective-permute-start | bytes 49160 | tf_op jit(solution)/shard_map/while/body/eval_jaxpr/ppermute | solution.py:13
  409.5 6.9 collective-permute-start
  416.3 75.6 %collective-permute-start.1 = (f32[32,128]{1,0:T(8,128)S(1)}, f32[32,128]{1,0:T(8,128)S(1)}, u32[]{:S(2)}, u32[]{:S(2)}) collective-permute-start(f32[32,128]{1,0:T(8,128)S(1)} %copy.27), channel_id=1, source_target_pairs={{0,1},{1,2},{2,3},{3,4},{4,5},{5,6},{6,7},{7,8},{8,9},{9,10},{10,1... | collective-permute-start | bytes 49160 | tf_op jit(solution)/shard_map/while/body/eval_jaxpr/ppermute | solution.py:13
  490.0 6.9 collective-permute-start
  496.9 75.6 %collective-permute-start.1 = (f32[32,128]{1,0:T(8,128)S(1)}, f32[32,128]{1,0:T(8,128)S(1)}, u32[]{:S(2)}, u32[]{:S(2)}) collective-permute-start(f32[32,128]{1,0:T(8,128)S(1)} %copy.27), channel_id=1, source_target_pairs={{0,1},{1,2},{2,3},{3,4},{4,5},{5,6},{6,7},{7,8},{8,9},{9,10},{10,1... | collective-permute-start | bytes 49160 | tf_op jit(solution)/shard_map/while/body/eval_jaxpr/ppermute | solution.py:13
  570.5 6.9 collective-permute-start
  577.4 75.6 %collective-permute-start.1 = (f32[32,128]{1,0:T(8,128)S(1)}, f32[32,128]{1,0:T(8,128)S(1)}, u32[]{:S(2)}, u32[]{:S(2)}) collective-permute-start(f32[32,128]{1,0:T(8,128)S(1)} %copy.27), channel_id=1, source_target_pairs={{0,1},{1,2},{2,3},{3,4},{4,5},{5,6},{6,7},{7,8},{8,9},{9,10},{10,1... | collective-permute-start | bytes 49160 | tf_op jit(solution)/shard_map/while/body/eval_jaxpr/ppermute | solution.py:13
  657.9 75.6 %collective-permute-start.1 = (f32[32,128]{1,0:T(8,128)S(1)}, f32[32,128]{1,0:T(8,128)S(1)}, u32[]{:S(2)}, u32[]{:S(2)}) collective-permute-start(f32[32,128]{1,0:T(8,128)S(1)} %copy.27), channel_id=1, source_target_pairs={{0,1},{1,2},{2,3},{3,4},{4,5},{5,6},{6,7},{7,8},{8,9},{9,10},{10,1... | collective-permute-start | bytes 49160 | tf_op jit(solution)/shard_map/while/body/eval_jaxpr/ppermute | solution.py:13
  738.4 75.6 %collective-permute-start.1 = (f32[32,128]{1,0:T(8,128)S(1)}, f32[32,128]{1,0:T(8,128)S(1)}, u32[]{:S(2)}, u32[]{:S(2)}) collective-permute-start(f32[32,128]{1,0:T(8,128)S(1)} %copy.27), channel_id=1, source_target_pairs={{0,1},{1,2},{2,3},{3,4},{4,5},{5,6},{6,7},{7,8},{8,9},{9,10},{10,1... | collective-permute-start | bytes 49160 | tf_op jit(solution)/shard_map/while/body/eval_jaxpr/ppermute | solution.py:13
  818.9 75.6 %collective-permute-start.1 = (f32[32,128]{1,0:T(8,128)S(1)}, f32[32,128]{1,0:T(8,128)S(1)}, u32[]{:S(2)}, u32[]{:S(2)}) collective-permute-start(f32[32,128]{1,0:T(8,128)S(1)} %copy.27), channel_id=1, source_target_pairs={{0,1},{1,2},{2,3},{3,4},{4,5},{5,6},{6,7},{7,8},{8,9},{9,10},{10,1... | collective-permute-start | bytes 49160 | tf_op jit(solution)/shard_map/while/body/eval_jaxpr/ppermute | solution.py:13
  892.6 6.9 collective-permute-start
  899.5 75.6 %collective-permute-start.1 = (f32[32,128]{1,0:T(8,128)S(1)}, f32[32,128]{1,0:T(8,128)S(1)}, u32[]{:S(2)}, u32[]{:S(2)}) collective-permute-start(f32[32,128]{1,0:T(8,128)S(1)} %copy.27), channel_id=1, source_target_pairs={{0,1},{1,2},{2,3},{3,4},{4,5},{5,6},{6,7},{7,8},{8,9},{9,10},{10,1... | collective-permute-start | bytes 49160 | tf_op jit(solution)/shard_map/while/body/eval_jaxpr/ppermute | solution.py:13
  980.0 75.6 %collective-permute-start.1 = (f32[32,128]{1,0:T(8,128)S(1)}, f32[32,128]{1,0:T(8,128)S(1)}, u32[]{:S(2)}, u32[]{:S(2)}) collective-permute-start(f32[32,128]{1,0:T(8,128)S(1)} %copy.27), channel_id=1, source_target_pairs={{0,1},{1,2},{2,3},{3,4},{4,5},{5,6},{6,7},{7,8},{8,9},{9,10},{10,1... | collective-permute-start | bytes 49160 | tf_op jit(solution)/shard_map/while/body/eval_jaxpr/ppermute | solution.py:13
  1053.6 6.9 collective-permute-start
  1060.5 75.6 %collective-permute-start.1 = (f32[32,128]{1,0:T(8,128)S(1)}, f32[32,128]{1,0:T(8,128)S(1)}, u32[]{:S(2)}, u32[]{:S(2)}) collective-permute-start(f32[32,128]{1,0:T(8,128)S(1)} %copy.27), channel_id=1, source_target_pairs={{0,1},{1,2},{2,3},{3,4},{4,5},{5,6},{6,7},{7,8},{8,9},{9,10},{10,1... | collective-permute-start | bytes 49160 | tf_op jit(solution)/shard_map/while/body/eval_jaxpr/ppermute | solution.py:13
  1141.0 75.6 %collective-permute-start.1 = (f32[32,128]{1,0:T(8,128)S(1)}, f32[32,128]{1,0:T(8,128)S(1)}, u32[]{:S(2)}, u32[]{:S(2)}) collective-permute-start(f32[32,128]{1,0:T(8,128)S(1)} %copy.27), channel_id=1, source_target_pairs={{0,1},{1,2},{2,3},{3,4},{4,5},{5,6},{6,7},{7,8},{8,9},{9,10},{10,1... | collective-permute-start | bytes 49160 | tf_op jit(solution)/shard_map/while/body/eval_jaxpr/ppermute | solution.py:13
  1221.5 75.6 %collective-permute-start.1 = (f32[32,128]{1,0:T(8,128)S(1)}, f32[32,128]{1,0:T(8,128)S(1)}, u32[]{:S(2)}, u32[]{:S(2)}) collective-permute-start(f32[32,128]{1,0:T(8,128)S(1)} %copy.27), channel_id=1, source_target_pairs={{0,1},{1,2},{2,3},{3,4},{4,5},{5,6},{6,7},{7,8},{8,9},{9,10},{10,1... | collective-permute-start | bytes 49160 | tf_op jit(solution)/shard_map/while/body/eval_jaxpr/ppermute | solution.py:13
  1302.1 75.6 %collective-permute-start.1 = (f32[32,128]{1,0:T(8,128)S(1)}, f32[32,128]{1,0:T(8,128)S(1)}, u32[]{:S(2)}, u32[]{:S(2)}) collective-permute-start(f32[32,128]{1,0:T(8,128)S(1)} %copy.27), channel_id=1, source_target_pairs={{0,1},{1,2},{2,3},{3,4},{4,5},{5,6},{6,7},{7,8},{8,9},{9,10},{10,1... | collective-permute-start | bytes 49160 | tf_op jit(solution)/shard_map/while/body/eval_jaxpr/ppermute | solution.py:13
  1375.7 6.9 collective-permute-start
  (14 other events, 296.7 us)
Sparse Core Ops, SparseCore 0:
  14.5 67.8 reduce-scatter.1
where the time goes:
time: 1390 us
  blocking collectives  1070 us (77%)
  waiting for transfers between devices  146 us (11%)
  starting transfers between devices  61.3 us (4%)
  matrix products  45.5 us (3%)
  loops' own time  32.3 us (2%)
  between operations  14.1 us (1%)
    psum x16, blocking collectives, run_section(): gradient = lax.psum(local_grad, 'samp')  1070 us
    ppermute x32, waiting for transfers between devices, from_behind(): return lax.ppermute(value, axis, pairs)  78.4 us
    reduce_scatter x1, waiting for transfers between devices, per_device(): lax.psum_scatter(partial_sum, 'feat', scatter_dimension=0, tiled=True)  68.1 us
    ppermute x32, starting transfers between devices, from_behind(): return lax.ppermute(value, axis, pairs)  61.3 us
    another operation x1, loops' own time, per_device(): lax.fori_loop(0, cycle_size, run_section, (blocks, residual, weight))  32.3 us
  transfers between devices with their start and end apart: 33, of which 17 were waited for; matrix products, arithmetic and copies ran while one was open for 4% of the time, Pallas kernels for 0%

commit v1 on v0

--- a/solution.py
+++ b/solution.py
@@ -55,7 +55,7 @@
         local_grad = jnp.einsum(
             "krc,kr->c", values, resid_tiles, preferred_element_type=jnp.float32
         )
-        gradient = lax.psum(local_grad, "samp")
+        gradient = jnp.sum(lax.all_gather(local_grad, "samp"), axis=0)
         current = lax.dynamic_index_in_dim(blocks, target, 0, keepdims=False)
         moved_block = current + jnp.dot(inverse, gradient, precision=exact_prec)
         shrunk = jnp.sign(moved_block) * jnp.maximum(jnp.abs(moved_block) - l1_penalty, 0.0)

time: 1390 us -> 959 us (0.69)
  blocking collectives: 1070 us -> 633 us
    psum x16 -> x0, blocking collectives: 1070 us -> none  [run_section(): gradient = lax.psum(local_grad, 'samp')]
    all_gather x0 -> x16, blocking collectives: none -> 633 us  [run_section(): gradient = jnp.sum(lax.all_gather(local_grad, 'samp'), axis=0)]
  transfers between devices with their start and end apart: 33 -> 33, of which waited for: 17 -> 17; matrix products, arithmetic and copies ran while one was open for 4% -> 7% of each run, Pallas kernels for 0% -> 0%
where the time goes in v1:
time: 959 us; the launch traced here: 957 us
  blocking collectives  633 us (66%)
  waiting for transfers between devices  144 us (15%)
  starting transfers between devices  61.3 us (6%)
  matrix products  45.4 us (5%)
  loops' own time  32.3 us (3%)
  between operations  14.1 us (1%)
  other arithmetic  13.4 us (1%)
  local copies, waits for them, and re-layouts  12.5 us (1%)
    all_gather x16, blocking collectives, run_section(): gradient = jnp.sum(lax.all_gather(local_grad, 'samp'), axis=0)  633 us
    ppermute x32, waiting for transfers between devices, from_behind(): return lax.ppermute(value, axis, pairs)  76.1 us
    reduce_scatter x1, waiting for transfers between devices, per_device(): lax.psum_scatter(partial_sum, 'feat', scatter_dimension=0, tiled=True)  68.1 us
    ppermute x32, starting transfers between devices, from_behind(): return lax.ppermute(value, axis, pairs)  61.3 us
    another operation x1, loops' own time, per_device(): lax.fori_loop(0, cycle_size, run_section, (blocks, residual, weight))  32.3 us
  transfers between devices with their start and end apart: 33, of which 17 were waited for; matrix products, arithmetic and copies ran while one was open for 7% of the time, Pallas kernels for 0%

profile of v1, /device:TPU:1, one launch (start us, length us, event | category | flops | bytes accessed | tf_op | source)
XLA Modules:
  0.0 956.7 jit_solution(13155265390092735043)
XLA Ops:
  14.4 68.1 %reduce-scatter.2.cloned.1.call-done = f32[32,128]{1,0:T(8,128)} async-done(((f32[512,128]{1,0:T(8,128)}), f32[32,128]{1,0:T(8,128)}) %reduce-scatter.2.cloned.1.call-update) | async-done | bytes 16400 | tf_op jit(solution)/shard_map/reduce_scatter | solution.py:32
  83.2 865.9 %while.20 = (s32[]{:T(128)}, f32[512,128]{1,0:T(8,128)S(1)}, f32[32,128]{1,0:T(8,128)S(1)}, f32[32,128]{1,0:T(8,128)S(1)}, s32[16]{0:T(128)S(1)}, /*index=5*/f32...) while((s32[]{:T(128)}, f32[512,128]{1,0:T(8,128)S(1)}, ...), condition=%wide.region_3.4_spmd.clone, body=%wide.region_1.3_spmd.clone.sunk | while | flops 8094994 | bytes 4627832 | solution.py:70
  88.4 53.7 %all-gather.4 = f32[32,1,128]{2,1,0:T(1,128)S(1)} all-gather(f32[1,1,128]{2,1,0:T(1,128)S(1)} %convolution_bitcast_fusion.3), channel_id=2, replica_groups=mesh['samp'=32,'feat'=16] {'samp'}, dimensions={0}, use_global_device_ids=true | all-gather | bytes 16896 | tf_op jit(solution)/shard_map/while/body/eval_jaxpr/all_gather | solution.py:58
  156.4 37.6 %all-gather.4 = f32[32,1,128]{2,1,0:T(1,128)S(1)} all-gather(f32[1,1,128]{2,1,0:T(1,128)S(1)} %convolution_bitcast_fusion.3), channel_id=2, replica_groups=mesh['samp'=32,'feat'=16] {'samp'}, dimensions={0}, use_global_device_ids=true | all-gather | bytes 16896 | tf_op jit(solution)/shard_map/while/body/eval_jaxpr/all_gather | solution.py:58
  198.7 4.9 collective-permute-done
  208.7 39.9 %all-gather.4 = f32[32,1,128]{2,1,0:T(1,128)S(1)} all-gather(f32[1,1,128]{2,1,0:T(1,128)S(1)} %convolution_bitcast_fusion.3), channel_id=2, replica_groups=mesh['samp'=32,'feat'=16] {'samp'}, dimensions={0}, use_global_device_ids=true | all-gather | bytes 16896 | tf_op jit(solution)/shard_map/while/body/eval_jaxpr/all_gather | solution.py:58
  262.9 37.6 %all-gather.4 = f32[32,1,128]{2,1,0:T(1,128)S(1)} all-gather(f32[1,1,128]{2,1,0:T(1,128)S(1)} %convolution_bitcast_fusion.3), channel_id=2, replica_groups=mesh['samp'=32,'feat'=16] {'samp'}, dimensions={0}, use_global_device_ids=true | all-gather | bytes 16896 | tf_op jit(solution)/shard_map/while/body/eval_jaxpr/all_gather | solution.py:58
  305.2 4.9 collective-permute-done
  315.2 39.9 %all-gather.4 = f32[32,1,128]{2,1,0:T(1,128)S(1)} all-gather(f32[1,1,128]{2,1,0:T(1,128)S(1)} %convolution_bitcast_fusion.3), channel_id=2, replica_groups=mesh['samp'=32,'feat'=16] {'samp'}, dimensions={0}, use_global_device_ids=true | all-gather | bytes 16896 | tf_op jit(solution)/shard_map/while/body/eval_jaxpr/all_gather | solution.py:58
  369.5 37.6 %all-gather.4 = f32[32,1,128]{2,1,0:T(1,128)S(1)} all-gather(f32[1,1,128]{2,1,0:T(1,128)S(1)} %convolution_bitcast_fusion.3), channel_id=2, replica_groups=mesh['samp'=32,'feat'=16] {'samp'}, dimensions={0}, use_global_device_ids=true | all-gather | bytes 16896 | tf_op jit(solution)/shard_map/while/body/eval_jaxpr/all_gather | solution.py:58
  411.7 4.9 collective-permute-done
  421.7 39.9 %all-gather.4 = f32[32,1,128]{2,1,0:T(1,128)S(1)} all-gather(f32[1,1,128]{2,1,0:T(1,128)S(1)} %convolution_bitcast_fusion.3), channel_id=2, replica_groups=mesh['samp'=32,'feat'=16] {'samp'}, dimensions={0}, use_global_device_ids=true | all-gather | bytes 16896 | tf_op jit(solution)/shard_map/while/body/eval_jaxpr/all_gather | solution.py:58
  476.0 37.6 %all-gather.4 = f32[32,1,128]{2,1,0:T(1,128)S(1)} all-gather(f32[1,1,128]{2,1,0:T(1,128)S(1)} %convolution_bitcast_fusion.3), channel_id=2, replica_groups=mesh['samp'=32,'feat'=16] {'samp'}, dimensions={0}, use_global_device_ids=true | all-gather | bytes 16896 | tf_op jit(solution)/shard_map/while/body/eval_jaxpr/all_gather | solution.py:58
  528.2 39.9 %all-gather.4 = f32[32,1,128]{2,1,0:T(1,128)S(1)} all-gather(f32[1,1,128]{2,1,0:T(1,128)S(1)} %convolution_bitcast_fusion.3), channel_id=2, replica_groups=mesh['samp'=32,'feat'=16] {'samp'}, dimensions={0}, use_global_device_ids=true | all-gather | bytes 16896 | tf_op jit(solution)/shard_map/while/body/eval_jaxpr/all_gather | solution.py:58
  582.5 37.6 %all-gather.4 = f32[32,1,128]{2,1,0:T(1,128)S(1)} all-gather(f32[1,1,128]{2,1,0:T(1,128)S(1)} %convolution_bitcast_fusion.3), channel_id=2, replica_groups=mesh['samp'=32,'feat'=16] {'samp'}, dimensions={0}, use_global_device_ids=true | all-gather | bytes 16896 | tf_op jit(solution)/shard_map/while/body/eval_jaxpr/all_gather | solution.py:58
  634.7 39.9 %all-gather.4 = f32[32,1,128]{2,1,0:T(1,128)S(1)} all-gather(f32[1,1,128]{2,1,0:T(1,128)S(1)} %convolution_bitcast_fusion.3), channel_id=2, replica_groups=mesh['samp'=32,'feat'=16] {'samp'}, dimensions={0}, use_global_device_ids=true | all-gather | bytes 16896 | tf_op jit(solution)/shard_map/while/body/eval_jaxpr/all_gather | solution.py:58
  689.0 37.6 %all-gather.4 = f32[32,1,128]{2,1,0:T(1,128)S(1)} all-gather(f32[1,1,128]{2,1,0:T(1,128)S(1)} %convolution_bitcast_fusion.3), channel_id=2, replica_groups=mesh['samp'=32,'feat'=16] {'samp'}, dimensions={0}, use_global_device_ids=true | all-gather | bytes 16896 | tf_op jit(solution)/shard_map/while/body/eval_jaxpr/all_gather | solution.py:58
  731.3 4.9 collective-permute-done
  741.3 39.9 %all-gather.4 = f32[32,1,128]{2,1,0:T(1,128)S(1)} all-gather(f32[1,1,128]{2,1,0:T(1,128)S(1)} %convolution_bitcast_fusion.3), channel_id=2, replica_groups=mesh['samp'=32,'feat'=16] {'samp'}, dimensions={0}, use_global_device_ids=true | all-gather | bytes 16896 | tf_op jit(solution)/shard_map/while/body/eval_jaxpr/all_gather | solution.py:58
  795.5 37.6 %all-gather.4 = f32[32,1,128]{2,1,0:T(1,128)S(1)} all-gather(f32[1,1,128]{2,1,0:T(1,128)S(1)} %convolution_bitcast_fusion.3), channel_id=2, replica_groups=mesh['samp'=32,'feat'=16] {'samp'}, dimensions={0}, use_global_device_ids=true | all-gather | bytes 16896 | tf_op jit(solution)/shard_map/while/body/eval_jaxpr/all_gather | solution.py:58
  837.8 4.9 collective-permute-done
  847.8 39.9 %all-gather.4 = f32[32,1,128]{2,1,0:T(1,128)S(1)} all-gather(f32[1,1,128]{2,1,0:T(1,128)S(1)} %convolution_bitcast_fusion.3), channel_id=2, replica_groups=mesh['samp'=32,'feat'=16] {'samp'}, dimensions={0}, use_global_device_ids=true | all-gather | bytes 16896 | tf_op jit(solution)/shard_map/while/body/eval_jaxpr/all_gather | solution.py:58
  902.0 37.6 %all-gather.4 = f32[32,1,128]{2,1,0:T(1,128)S(1)} all-gather(f32[1,1,128]{2,1,0:T(1,128)S(1)} %convolution_bitcast_fusion.3), channel_id=2, replica_groups=mesh['samp'=32,'feat'=16] {'samp'}, dimensions={0}, use_global_device_ids=true | all-gather | bytes 16896 | tf_op jit(solution)/shard_map/while/body/eval_jaxpr/all_gather | solution.py:58
  944.3 4.9 collective-permute-done
  (241 shorter events, 179.4 us)
Async XLA Ops:
  7.2 75.3 %reduce-scatter.2.cloned.1.call-start = ((), (), s32[]{:S(2)}) async-start(), calls=%async_computation.1 | async-start | bytes 278528 | tf_op jit(solution)/shard_map/reduce_scatter | solution.py:32
  83.3 63.5 %collective-permute-start.1 = (f32[32,128]{1,0:T(8,128)S(1)}, f32[32,128]{1,0:T(8,128)S(1)}, u32[]{:S(2)}, u32[]{:S(2)}) collective-permute-start(f32[32,128]{1,0:T(8,128)S(1)} %copy.27), channel_id=1, source_target_pairs={{0,1},{1,2},{2,3},{3,4},{4,5},{5,6},{6,7},{7,8},{8,9},{9,10},{10,1... | collective-permute-start | bytes 49160 | tf_op jit(solution)/shard_map/while/body/eval_jaxpr/ppermute | solution.py:13
  151.4 47.4 %collective-permute-start.1 = (f32[32,128]{1,0:T(8,128)S(1)}, f32[32,128]{1,0:T(8,128)S(1)}, u32[]{:S(2)}, u32[]{:S(2)}) collective-permute-start(f32[32,128]{1,0:T(8,128)S(1)} %copy.27), channel_id=1, source_target_pairs={{0,1},{1,2},{2,3},{3,4},{4,5},{5,6},{6,7},{7,8},{8,9},{9,10},{10,1... | collective-permute-start | bytes 49160 | tf_op jit(solution)/shard_map/while/body/eval_jaxpr/ppermute | solution.py:13
  196.7 6.9 collective-permute-start
  203.6 49.6 %collective-permute-start.1 = (f32[32,128]{1,0:T(8,128)S(1)}, f32[32,128]{1,0:T(8,128)S(1)}, u32[]{:S(2)}, u32[]{:S(2)}) collective-permute-start(f32[32,128]{1,0:T(8,128)S(1)} %copy.27), channel_id=1, source_target_pairs={{0,1},{1,2},{2,3},{3,4},{4,5},{5,6},{6,7},{7,8},{8,9},{9,10},{10,1... | collective-permute-start | bytes 49160 | tf_op jit(solution)/shard_map/while/body/eval_jaxpr/ppermute | solution.py:13
  257.9 47.4 %collective-permute-start.1 = (f32[32,128]{1,0:T(8,128)S(1)}, f32[32,128]{1,0:T(8,128)S(1)}, u32[]{:S(2)}, u32[]{:S(2)}) collective-permute-start(f32[32,128]{1,0:T(8,128)S(1)} %copy.27), channel_id=1, source_target_pairs={{0,1},{1,2},{2,3},{3,4},{4,5},{5,6},{6,7},{7,8},{8,9},{9,10},{10,1... | collective-permute-start | bytes 49160 | tf_op jit(solution)/shard_map/while/body/eval_jaxpr/ppermute | solution.py:13
  303.3 6.9 collective-permute-start
  310.1 49.6 %collective-permute-start.1 = (f32[32,128]{1,0:T(8,128)S(1)}, f32[32,128]{1,0:T(8,128)S(1)}, u32[]{:S(2)}, u32[]{:S(2)}) collective-permute-start(f32[32,128]{1,0:T(8,128)S(1)} %copy.27), channel_id=1, source_target_pairs={{0,1},{1,2},{2,3},{3,4},{4,5},{5,6},{6,7},{7,8},{8,9},{9,10},{10,1... | collective-permute-start | bytes 49160 | tf_op jit(solution)/shard_map/while/body/eval_jaxpr/ppermute | solution.py:13
  364.4 47.4 %collective-permute-start.1 = (f32[32,128]{1,0:T(8,128)S(1)}, f32[32,128]{1,0:T(8,128)S(1)}, u32[]{:S(2)}, u32[]{:S(2)}) collective-permute-start(f32[32,128]{1,0:T(8,128)S(1)} %copy.27), channel_id=1, source_target_pairs={{0,1},{1,2},{2,3},{3,4},{4,5},{5,6},{6,7},{7,8},{8,9},{9,10},{10,1... | collective-permute-start | bytes 49160 | tf_op jit(solution)/shard_map/while/body/eval_jaxpr/ppermute | solution.py:13
  409.8 6.9 collective-permute-start
  416.6 49.6 %collective-permute-start.1 = (f32[32,128]{1,0:T(8,128)S(1)}, f32[32,128]{1,0:T(8,128)S(1)}, u32[]{:S(2)}, u32[]{:S(2)}) collective-permute-start(f32[32,128]{1,0:T(8,128)S(1)} %copy.27), channel_id=1, source_target_pairs={{0,1},{1,2},{2,3},{3,4},{4,5},{5,6},{6,7},{7,8},{8,9},{9,10},{10,1... | collective-permute-start | bytes 49160 | tf_op jit(solution)/shard_map/while/body/eval_jaxpr/ppermute | solution.py:13
  470.9 47.4 %collective-permute-start.1 = (f32[32,128]{1,0:T(8,128)S(1)}, f32[32,128]{1,0:T(8,128)S(1)}, u32[]{:S(2)}, u32[]{:S(2)}) collective-permute-start(f32[32,128]{1,0:T(8,128)S(1)} %copy.27), channel_id=1, source_target_pairs={{0,1},{1,2},{2,3},{3,4},{4,5},{5,6},{6,7},{7,8},{8,9},{9,10},{10,1... | collective-permute-start | bytes 49160 | tf_op jit(solution)/shard_map/while/body/eval_jaxpr/ppermute | solution.py:13
  516.3 6.9 collective-permute-start
  523.1 49.6 %collective-permute-start.1 = (f32[32,128]{1,0:T(8,128)S(1)}, f32[32,128]{1,0:T(8,128)S(1)}, u32[]{:S(2)}, u32[]{:S(2)}) collective-permute-start(f32[32,128]{1,0:T(8,128)S(1)} %copy.27), channel_id=1, source_target_pairs={{0,1},{1,2},{2,3},{3,4},{4,5},{5,6},{6,7},{7,8},{8,9},{9,10},{10,1... | collective-permute-start | bytes 49160 | tf_op jit(solution)/shard_map/while/body/eval_jaxpr/ppermute | solution.py:13
  577.4 47.4 %collective-permute-start.1 = (f32[32,128]{1,0:T(8,128)S(1)}, f32[32,128]{1,0:T(8,128)S(1)}, u32[]{:S(2)}, u32[]{:S(2)}) collective-permute-start(f32[32,128]{1,0:T(8,128)S(1)} %copy.27), channel_id=1, source_target_pairs={{0,1},{1,2},{2,3},{3,4},{4,5},{5,6},{6,7},{7,8},{8,9},{9,10},{10,1... | collective-permute-start | bytes 49160 | tf_op jit(solution)/shard_map/while/body/eval_jaxpr/ppermute | solution.py:13
  629.7 49.6 %collective-permute-start.1 = (f32[32,128]{1,0:T(8,128)S(1)}, f32[32,128]{1,0:T(8,128)S(1)}, u32[]{:S(2)}, u32[]{:S(2)}) collective-permute-start(f32[32,128]{1,0:T(8,128)S(1)} %copy.27), channel_id=1, source_target_pairs={{0,1},{1,2},{2,3},{3,4},{4,5},{5,6},{6,7},{7,8},{8,9},{9,10},{10,1... | collective-permute-start | bytes 49160 | tf_op jit(solution)/shard_map/while/body/eval_jaxpr/ppermute | solution.py:13
  683.9 47.4 %collective-permute-start.1 = (f32[32,128]{1,0:T(8,128)S(1)}, f32[32,128]{1,0:T(8,128)S(1)}, u32[]{:S(2)}, u32[]{:S(2)}) collective-permute-start(f32[32,128]{1,0:T(8,128)S(1)} %copy.27), channel_id=1, source_target_pairs={{0,1},{1,2},{2,3},{3,4},{4,5},{5,6},{6,7},{7,8},{8,9},{9,10},{10,1... | collective-permute-start | bytes 49160 | tf_op jit(solution)/shard_map/while/body/eval_jaxpr/ppermute | solution.py:13
  729.3 6.9 collective-permute-start
  736.2 49.6 %collective-permute-start.1 = (f32[32,128]{1,0:T(8,128)S(1)}, f32[32,128]{1,0:T(8,128)S(1)}, u32[]{:S(2)}, u32[]{:S(2)}) collective-permute-start(f32[32,128]{1,0:T(8,128)S(1)} %copy.27), channel_id=1, source_target_pairs={{0,1},{1,2},{2,3},{3,4},{4,5},{5,6},{6,7},{7,8},{8,9},{9,10},{10,1... | collective-permute-start | bytes 49160 | tf_op jit(solution)/shard_map/while/body/eval_jaxpr/ppermute | solution.py:13
  790.4 47.4 %collective-permute-start.1 = (f32[32,128]{1,0:T(8,128)S(1)}, f32[32,128]{1,0:T(8,128)S(1)}, u32[]{:S(2)}, u32[]{:S(2)}) collective-permute-start(f32[32,128]{1,0:T(8,128)S(1)} %copy.27), channel_id=1, source_target_pairs={{0,1},{1,2},{2,3},{3,4},{4,5},{5,6},{6,7},{7,8},{8,9},{9,10},{10,1... | collective-permute-start | bytes 49160 | tf_op jit(solution)/shard_map/while/body/eval_jaxpr/ppermute | solution.py:13
  835.8 6.9 collective-permute-start
  842.7 49.6 %collective-permute-start.1 = (f32[32,128]{1,0:T(8,128)S(1)}, f32[32,128]{1,0:T(8,128)S(1)}, u32[]{:S(2)}, u32[]{:S(2)}) collective-permute-start(f32[32,128]{1,0:T(8,128)S(1)} %copy.27), channel_id=1, source_target_pairs={{0,1},{1,2},{2,3},{3,4},{4,5},{5,6},{6,7},{7,8},{8,9},{9,10},{10,1... | collective-permute-start | bytes 49160 | tf_op jit(solution)/shard_map/while/body/eval_jaxpr/ppermute | solution.py:13
  896.9 47.4 %collective-permute-start.1 = (f32[32,128]{1,0:T(8,128)S(1)}, f32[32,128]{1,0:T(8,128)S(1)}, u32[]{:S(2)}, u32[]{:S(2)}) collective-permute-start(f32[32,128]{1,0:T(8,128)S(1)} %copy.27), channel_id=1, source_target_pairs={{0,1},{1,2},{2,3},{3,4},{4,5},{5,6},{6,7},{7,8},{8,9},{9,10},{10,1... | collective-permute-start | bytes 49160 | tf_op jit(solution)/shard_map/while/body/eval_jaxpr/ppermute | solution.py:13
  942.3 6.9 collective-permute-start
  (14 other events, 294.5 us)
Sparse Core Ops, SparseCore 0:
  14.5 67.8 reduce-scatter.1
